TPU v7x, 32 devices: a whole 2x2x4 slice. The times are simulated.
32 devices in a mesh: group: 4 (over y, x), seq: 8 (over z, core).
Axes of the slice: x: 2, y: 2, z: 4, core: 2. Of those that a mesh axis runs over, the one named last changes fastest.
Arguments:
- tokens: bfloat16 [32, 2048, 2048], P('group', 'seq'), may hold values from -6 to 6
- image_keys: bfloat16 [32, 256, 2048], P('group', 'seq'), may hold values from -256 to 256
- image_values: bfloat16 [32, 256, 2048], P('group', 'seq'), may hold values from -18 to 18
- text_len: int32 [32], replicated, may hold values from 1 to 2048
- image_len: int32 [32], replicated, may hold values from 1 to 256
- counts: int32 [6], replicated, may hold values from 1 to 4, as said below
- old_group: int32 [6], replicated, may hold values from 0 to 3, as said below
- new_group: int32 [6], replicated, may hold values from 0 to 3, as said below
- w_query: bfloat16 [2048, 2048], replicated, may hold values from -0.125 to 0.125
- w_out: bfloat16 [2048, 2048], replicated, may hold values from -0.125 to 0.125
Outputs:
- layer_out: bfloat16 [32, 2048, 2048], P('group', 'seq')
Inputs may be any that keep to these rules, and one draw needn't show every extreme that they name: `counts`: every task has at most 4 samples, and some task has exactly 4. `old_group`: each group is the old group of at most two tasks, and no two tasks share both their old group and their new group, so at most 4 samples go from one old group to one new group. `new_group`: each group is the new group of at most two tasks.
All inputs are finite; a program needn't handle non-finite values.
Results may differ from a plain program's by a relative error of at most 0.011.
Values may be sent and summed in bfloat16 or wider, within the bound.
A program may use at most 128 MiB of HBM per device.

v0:
```python
import jax
import jax.numpy as jnp
from jax import lax
from jax.sharding import PartitionSpec as P

HEAD_DIM = 128
HALF = 4
masked_score = -1e30
norm_eps = 1e-05


def layout(counts, old_group, new_group, group_count, slot_count):
    task_order = jnp.arange(counts.shape[0], dtype=jnp.int32)
    earlier = task_order[None, :] < task_order[:, None]
    same_old = old_group[None, :] == old_group[:, None]
    same_new = new_group[None, :] == new_group[:, None]
    old_start = jnp.sum(jnp.where(earlier & same_old, counts[None, :], 0), axis=1)
    new_start = jnp.sum(jnp.where(earlier & same_new, counts[None, :], 0), axis=1)
    target = jnp.arange(group_count * slot_count, dtype=jnp.int32)
    target_group = target // slot_count
    target_slot = target % slot_count
    matches = (
        (new_group[None, :] == target_group[:, None])
        & (target_slot[:, None] >= new_start[None, :])
        & (target_slot[:, None] < (new_start + counts)[None, :])
    )
    filled = jnp.any(matches, axis=1)
    offset = target_slot - jnp.sum(jnp.where(matches, new_start[None, :], 0), axis=1)
    source_group = jnp.sum(jnp.where(matches, old_group[None, :], 0), axis=1)
    source_slot = jnp.sum(jnp.where(matches, old_start[None, :], 0), axis=1) + offset
    return (filled, source_group, source_slot, offset, old_start)


def normalize(samples_rows):
    values = samples_rows.astype(jnp.float32)
    average = jnp.mean(values, axis=-1, keepdims=True)
    centred = values - average
    variance = jnp.mean(centred * centred, axis=-1, keepdims=True)
    return (centred * lax.rsqrt(variance + norm_eps)).astype(jnp.bfloat16)


def spread_rows(source_array, source_index, wanted):
    gathered = jnp.take(source_array, source_index, axis=0)
    return jnp.where(wanted[:, None, None], gathered, jnp.zeros((), source_array.dtype))


def regroup(joined, group_index, group_count, slot_count, tables, counts, old_group, new_group):
    filled, source_group, source_slot, offset, old_start = tables
    own_first = group_index * slot_count
    filled_here = lax.dynamic_slice_in_dim(filled, own_first, slot_count)
    from_group = lax.dynamic_slice_in_dim(source_group, own_first, slot_count)
    destinations = jnp.arange(group_count, dtype=jnp.int32)
    pairing = (old_group[None, :] == group_index) & (new_group[None, :] == destinations[:, None])
    pair_first = jnp.sum(jnp.where(pairing, old_start[None, :], 0), axis=1)
    pair_amount = jnp.sum(jnp.where(pairing, counts[None, :], 0), axis=1)
    position = jnp.arange(HALF, dtype=jnp.int32)
    sending = (position[None, :] < pair_amount[:, None]).reshape(-1)
    source_index = jnp.where(sending, (pair_first[:, None] + position[None, :]).reshape(-1), 0)
    outgoing = spread_rows(joined, source_index, sending)
    incoming = lax.all_to_all(outgoing, "group", split_axis=0, concat_axis=0, tiled=True)
    chosen = from_group * HALF + lax.dynamic_slice_in_dim(offset, own_first, slot_count)
    chosen = jnp.where(filled_here, chosen, 0)
    return spread_rows(incoming, chosen, filled_here)


def cross_layer(
    samples_rows, key_rows, value_rows, text_limit, key_limit, w_query, w_out, first_row
):
    slot_count, row_count, feature_count = samples_rows.shape
    head_count = w_query.shape[1] // HEAD_DIM
    normal = normalize(samples_rows).reshape(slot_count * row_count, feature_count)
    queries = (
        jnp.dot(normal, w_query, preferred_element_type=jnp.float32) * HEAD_DIM ** (-0.5)
    ).astype(jnp.bfloat16)
    queries = queries.reshape(slot_count, row_count, head_count, HEAD_DIM)
    running_max = jnp.full((slot_count, head_count, row_count), masked_score, jnp.float32)
    piece_keys = lax.all_gather(key_rows, "seq", axis=1, tiled=True)
    piece_values = lax.all_gather(value_rows, "seq", axis=1, tiled=True)
    key_count = piece_keys.shape[1]
    head_keys = piece_keys.reshape(slot_count, key_count, head_count, HEAD_DIM)
    head_values = piece_values.reshape(slot_count, key_count, head_count, HEAD_DIM)
    scores = jnp.einsum("sqhd,skhd->shqk", queries, head_keys, preferred_element_type=jnp.float32)
    position = jnp.arange(key_count, dtype=jnp.int32)
    allowed = (position[None, :] < key_limit[:, None])[:, None, None, :]
    scores = jnp.where(allowed, scores, masked_score)
    new_max = jnp.maximum(running_max, jnp.max(scores, axis=-1))
    probs = jnp.where(allowed, jnp.exp(scores - new_max[..., None]), 0.0)
    running_sum = jnp.sum(probs, axis=-1)
    weights = probs.astype(jnp.bfloat16)
    running_ctx = jnp.einsum(
        "shqk,skhd->shqd", weights, head_values, preferred_element_type=jnp.float32
    )
    running_max, running_sum, running_ctx = (new_max, running_sum, running_ctx)
    context = running_ctx / running_sum[..., None]
    context = (
        context.transpose(0, 2, 1, 3)
        .reshape(slot_count * row_count, head_count * HEAD_DIM)
        .astype(jnp.bfloat16)
    )
    projected = jnp.dot(context, w_out, preferred_element_type=jnp.float32).reshape(
        slot_count, row_count, feature_count
    )
    row_position = first_row + jnp.arange(row_count, dtype=jnp.int32)
    kept_rows = row_position[None, :] < text_limit[:, None]
    return jnp.where(kept_rows[..., None], projected, 0.0).astype(jnp.bfloat16)


def on_device(
    tokens,
    image_keys,
    image_values,
    text_len,
    image_len,
    counts,
    old_group,
    new_group,
    w_query,
    w_out,
):
    group_count = lax.axis_size("group")
    slot_count = tokens.shape[0]
    row_count = tokens.shape[1]
    group_index = lax.axis_index("group")
    first_row = lax.axis_index("seq") * row_count
    tables = layout(counts, old_group, new_group, group_count, slot_count)
    own_first = group_index * slot_count
    text_limit = lax.dynamic_slice_in_dim(text_len, own_first, slot_count)
    key_limit = lax.dynamic_slice_in_dim(image_len, own_first, slot_count)
    attended = cross_layer(
        tokens, image_keys, image_values, text_limit, key_limit, w_query, w_out, first_row
    )
    return regroup(
        attended, group_index, group_count, slot_count, tables, counts, old_group, new_group
    )


def solution(mesh):
    in_specs = (
        P("group", "seq", None),
        P("group", "seq", None),
        P("group", "seq", None),
        P(),
        P(),
        P(),
        P(),
        P(),
        P(),
        P(),
    )
    out_specs = P("group", "seq", None)
    return jax.shard_map(
        on_device, mesh=mesh, in_specs=in_specs, out_specs=out_specs, check_vma=False
    )
```

profile of v0, /device:TPU:0, one launch (start us, length us, event | category | flops | bytes accessed | tf_op | source)
XLA Modules:
  0.0 466.5 jit_solution(17421429270864026179)
XLA Ops:
  6.5 2.9 copy.28
  9.5 0.7 all-gather.5.cloned.1.call-update
  10.2 4.7 %convert_reduce_fusion = f32[8,256]{1,0:T(8,128)S(1)} fusion(bf16[8,256,2048]{2,1,0:T(8,128)(2,1)} %param.10), kind=kLoop, calls=%fused_computation.7 | loop fusion | flops 8386560 | bytes 8396800 | tf_op jit(solution)/shard_map/reduce_sum | solution.py:36
  14.9 1.1 copy-done
  16.0 2.4 fusion.4
  18.3 2.5 fusion.5
  21.0 19.4 %fusion.21 = bf16[256,8,16,128]{3,1,2,0:T(8,128)(2,1)} fusion(bf16[2048,2048]{1,0:T(8,128)(2,1)S(1)} %bitcast.27, bf16[2048,2048]{1,0:T(8,128)(2,1)S(1)} %bitcast.31), kind=kOutput, calls=%fused_computation.27 | convolution fusion | flops 17188257792 | bytes 25165824 | tf_op jit(solution)/shard_map/dot_general | solution.py:73
  40.3 9.8 %copy.38 = bf16[256,8,16,128]{3,2,1,0:T(8,128)(2,1)} copy(bf16[256,8,16,128]{3,1,2,0:T(8,128)(2,1)} %fusion.21) | data formatting | bytes 16777216
  50.3 0.2 select_reduce_fusion.4
  50.5 0.2 select_reduce_fusion.6
  51.3 43.1 %all-gather.3.cloned.1.call-done = bf16[8,256,2048]{2,0,1:T(8,128)(2,1)} async-done(((bf16[8,32,2048]{2,0,1:T(8,128)(2,1)}), bf16[8,256,2048]{2,0,1:T(8,128)(2,1)}) %all-gather.3.cloned.1.call-update) | async-done | bytes 8388624 | tf_op jit(solution)/shard_map/all_gather | solution.py:77
  94.3 13.0 %copy.29 = bf16[8,256,2048]{1,2,0:T(8,128)(2,1)} copy(bf16[8,256,2048]{2,0,1:T(8,128)(2,1)} %all-gather.3.cloned.1.call-done) | data formatting | bytes 16777216 | tf_op jit(solution)/shard_map/all_gather | solution.py:77
  107.3 21.7 %select_reduce_fusion = (f32[8,16,256]{2,1,0:T(8,128)S(1)}, f32[8,16,256,256]{2,3,1,0:T(8,128)}) fusion(pred[8,256]{1,0:T(8,128)(4,1)S(1)} %iota_compare_fusion, bf16[8,256,16,128]{1,3,2,0:T(8,128)(2,1)} %bitcast.26, bf16[8,256,16,128]{3,2,1,0:T(8,128)(2,1)} %bitcast.25), kind=kOutput, calls=%fused_computation.3 | convolution fusion | flops 2164228096 | bytes 50464768 | tf_op jit(solution)/shard_map/sqhd,skhd->shqk/dot_general | solution.py:82
  129.1 14.7 %fusion = f32[8,16,256]{2,1,0:T(8,128)S(1)} fusion(f32[8,16,256,256]{2,3,1,0:T(8,128)} %get-tuple-element.18, f32[8,16,256]{2,1,0:T(8,128)S(1)} %broadcast_maximum_fusion, pred[8,256]{1,0:T(8,128)(4,1)S(1)} %iota_compare_fusion), kind=kLoop, calls=%fused_computation.4 | loop fusion | flops 33521664 | bytes 33818624 | tf_op jit(solution)/shard_map/reduce_sum | solution.py:88
  143.8 32.7 %all-gather.5.cloned.1.call-done = bf16[8,256,2048]{2,1,0:T(8,128)(2,1)} async-done(((bf16[8,32,2048]{2,1,0:T(8,128)(2,1)}), bf16[8,256,2048]{2,1,0:T(8,128)(2,1)}) %all-gather.5.cloned.1.call-update) | async-done | bytes 8388624 | tf_op jit(solution)/shard_map/all_gather | solution.py:78
  176.5 11.3 %copy.32 = bf16[8,256,2048]{1,2,0:T(8,128)(2,1)} copy(bf16[8,256,2048]{2,1,0:T(8,128)(2,1)} %all-gather.5.cloned.1.call-done) | data formatting | bytes 16777216 | tf_op jit(solution)/shard_map/all_gather | solution.py:78
  187.8 17.3 %fusion.8 = bf16[8,256,16,128]{1,3,2,0:T(8,128)(2,1)S(1)} fusion(f32[8,256,16]{1,2,0:T(8,128)S(1)} %bitcast.29, bf16[8,256,16,128]{1,3,2,0:T(8,128)(2,1)} %bitcast.28, f32[8,16,256,256]{2,3,1,0:T(8,128)} %get-tuple-element.18, f32[8,16,256]{2,1,0:T(8,128)S(1)} %broadcast_maximum_fusion, pred[8,256]{1,0:T(8,128)(4,1)S(1)} %iota_compare_fusion), kind=kOutput, calls=%fused_computation.14 | convolution fusion | flops 2189426688 | bytes 50595840 | tf_op jit(solution)/shard_map/shqk,skhd->shqd/dot_general | solution.py:90
  205.1 21.7 %select_convert_fusion = bf16[8,256,2048]{2,1,0:T(8,128)(2,1)} fusion(pred[8,256]{1,0:T(8,128)(4,1)S(1)} %broadcast_compare_fusion, bf16[8,256,2048]{1,2,0:T(8,128)(2,1)S(1)} %bitcast.32, bf16[2048,2048]{1,0:T(8,128)(2,1)} %param.19), kind=kOutput, calls=%fused_computation.16 | convolution fusion | flops 17188257792 | bytes 25167872 | tf_op jit(solution)/shard_map/dot_general | solution.py:100
  226.8 10.3 %gather_fusion = bf16[16,256,2048]{2,1,0:T(8,128)(2,1)} fusion(bf16[8,256,2048]{2,1,0:T(8,128)(2,1)} %select_convert_fusion, s32[1024]{0:T(1024)S(1)} %pad_clamp_fusion.1), kind=kCustom, calls=%fused_computation | custom fusion | bytes 33554496 | tf_op jit(solution)/shard_map/jit(_take)/gather | solution.py:43
  237.1 14.3 %select_select_fusion = bf16[16,256,2048]{2,1,0:T(8,128)(2,1)} fusion(bf16[16,256,2048]{2,1,0:T(8,128)(2,1)} %gather_fusion, pred[16]{0:T(512)(128)(4,1)S(1)} %compare_and_fusion.1, pred[16]{0:T(512)(128)(4,1)S(1)} %lt.144), kind=kLoop, calls=%fused_computation.15 | loop fusion | flops 16777216 | bytes 33554464 | tf_op jit(solution)/shard_map/jit(_where)/select_n | solution.py:44
  251.4 7.0 %all-to-all-start = ((bf16[16,256,2048]{2,1,0:T(8,128)(2,1)}), bf16[16,256,2048]{2,1,0:T(8,128)(2,1)}, u32[]{:S(2)}, u32[]{:S(2)}) async-start(bf16[16,256,2048]{2,1,0:T(8,128)(2,1)} %select_select_fusion), calls=%async_computation | async-start | bytes 33554432 | tf_op jit(solution)/shard_map/all_to_all | solution.py:60
  258.6 182.7 %all-to-all-done = bf16[16,256,2048]{2,1,0:T(8,128)(2,1)} async-done(((bf16[16,256,2048]{2,1,0:T(8,128)(2,1)}), bf16[16,256,2048]{2,1,0:T(8,128)(2,1)}, u32[]{:S(2)}, u32[]{:S(2)}) %all-to-all-start) | async-done | bytes 16777248 | tf_op jit(solution)/shard_map/all_to_all | solution.py:60
  441.3 10.6 %gather_fusion.1 = bf16[8,256,2048]{2,1,0:T(8,128)(2,1)} fusion(bf16[16,256,2048]{2,1,0:T(8,128)(2,1)} %all-to-all-done, s32[1024]{0:T(1024)S(1)} %pad_clamp_fusion), kind=kCustom, calls=%fused_computation.1 | custom fusion | bytes 16777248 | tf_op jit(solution)/shard_map/jit(_take)/gather | solution.py:43
  451.9 7.7 %select_select_fusion.1 = bf16[8,256,2048]{2,1,0:T(8,128)(2,1)} fusion(bf16[8,256,2048]{2,1,0:T(8,128)(2,1)} %gather_fusion.1, pred[8]{0:T(512)(128)(4,1)S(1)} %get-tuple-element.11, pred[8]{0:T(512)(128)(4,1)S(1)} %get-tuple-element.13), kind=kLoop, calls=%fused_computation.26 | loop fusion | flops 8388608 | bytes 16777232 | tf_op jit(solution)/shard_map/jit(_where)/select_n | solution.py:44
  (43 shorter events, 1.1 us)
Async XLA Ops:
  6.5 87.8 %all-gather.3.cloned.1.call-start = ((), (), s32[]{:S(2)}) async-start(), calls=%async_computation.1 | async-start | bytes 9437184 | tf_op jit(solution)/shard_map/all_gather | solution.py:77
  9.4 167.1 %all-gather.5.cloned.1.call-start = ((), (), s32[]{:S(2)}) async-start(), calls=%async_computation.2 | async-start | bytes 9437184 | tf_op jit(solution)/shard_map/all_gather | solution.py:78
  10.2 5.8 %copy-start = (bf16[8,256,2048]{2,1,0:T(8,128)(2,1)S(1)}, bf16[8,256,2048]{2,1,0:T(8,128)(2,1)}, u32[]{:S(2)}) copy-start(bf16[8,256,2048]{2,1,0:T(8,128)(2,1)} %param.10) | copy-start | bytes 25165828
  16.0 4.9 %slice-start = ((s8[8388608]{0:T(1024)(128)(4,1)}), s8[4194304]{0:T(1024)(128)(4,1)S(1)}, s32[]{:S(2)}) async-start(s8[8388608]{0:T(1024)(128)(4,1)} %bitcast.30), calls=%async_computation.3 | async-start | bytes 8388608
  18.3 2.6 slice-start.1
  40.3 9.8 %copy-start.4 = (s32[32]{0:T(128)S(1)}, s32[32]{0:T(128)}, u32[]{:S(2)}) copy-start(s32[32]{0:T(128)} %param.14) | copy-start | bytes 388
  40.3 9.9 %copy-start.5 = (s32[32]{0:T(128)S(1)}, s32[32]{0:T(128)}, u32[]{:S(2)}) copy-start(s32[32]{0:T(128)} %param.13) | copy-start | bytes 388
  40.3 10.0 %copy-start.1 = (s32[6]{0:T(128)S(1)}, s32[6]{0:T(128)}, u32[]{:S(2)}) copy-start(s32[6]{0:T(128)} %param.17) | copy-start | bytes 76
  40.3 10.0 %copy-start.2 = (s32[6]{0:T(128)S(1)}, s32[6]{0:T(128)}, u32[]{:S(2)}) copy-start(s32[6]{0:T(128)} %param.16) | copy-start | bytes 76
  40.3 10.0 %copy-start.3 = (s32[6]{0:T(128)S(1)}, s32[6]{0:T(128)}, u32[]{:S(2)}) copy-start(s32[6]{0:T(128)} %param.15) | copy-start | bytes 76
  251.4 189.9 %all-to-all-start = ((bf16[16,256,2048]{2,1,0:T(8,128)(2,1)}), bf16[16,256,2048]{2,1,0:T(8,128)(2,1)}, u32[]{:S(2)}, u32[]{:S(2)}) async-start(bf16[16,256,2048]{2,1,0:T(8,128)(2,1)} %select_select_fusion), calls=%async_computation | async-start | bytes 33554432 | tf_op jit(solution)/shard_map/all_to_all | solution.py:60
Sparse Core Ops, SparseCore 0:
  9.6 84.7 all-gather.2
  95.9 80.5 all-gather.4
where the time goes:
time: 468 us; the launch traced here: 466 us
  waiting for transfers between devices  259 us (55%)
  matrix products  80.1 us (17%)
  local copies, waits for them, and re-layouts  59.4 us (13%)
  other arithmetic  47.2 us (10%)
  between operations  13.6 us (3%)
  starting transfers between devices  7 us (1%)
    all_to_all x1, waiting for transfers between devices, regroup(): lax.all_to_all(outgoing, 'group', split_axis=0, concat_axis=0, tiled=True)  183 us
    all_gather x1, waiting for transfers between devices, cross_layer(): piece_keys = lax.all_gather(key_rows, 'seq', axis=1, tiled=True)  43.1 us
    all_gather x1, waiting for transfers between devices, cross_layer(): piece_values = lax.all_gather(value_rows, 'seq', axis=1, tiled=True)  32.7 us
    select_n x2, other arithmetic, spread_rows(): jnp.where(wanted[:, None, None], gathered, jnp.zeros((), source_array.dty...  22 us
    dot_general x1, matrix products, cross_layer(): jnp.einsum('sqhd,skhd->shqk', queries, head_keys, preferred_element_type=...  21.7 us
    dot_general x1, matrix products, cross_layer(): jnp.dot(context, w_out, preferred_element_type=jnp.float32)  21.7 us
    gather x2, local copies, waits for them, and re-layouts, spread_rows(): gathered = jnp.take(source_array, source_index, axis=0)  20.9 us
    dot_general x1, matrix products, cross_layer(): jnp.dot(normal, w_query, preferred_element_type=jnp.float32)  19.4 us
  transfers between devices with their start and end apart: 3, of which 3 were waited for; matrix products, arithmetic and copies ran while one was open for 19% of the time, Pallas kernels for 0%

commit v1 on v0

--- a/solution.py
+++ b/solution.py
@@ -74,8 +74,9 @@
     ).astype(jnp.bfloat16)
     queries = queries.reshape(slot_count, row_count, head_count, HEAD_DIM)
     running_max = jnp.full((slot_count, head_count, row_count), masked_score, jnp.float32)
-    piece_keys = lax.all_gather(key_rows, "seq", axis=1, tiled=True)
-    piece_values = lax.all_gather(value_rows, "seq", axis=1, tiled=True)
+    wide_out = jnp.concatenate([key_rows, value_rows], axis=0)
+    parts_out = lax.all_gather(wide_out, axis_name="seq", axis=1, tiled=True)
+    piece_keys, piece_values = jnp.split(parts_out, [key_rows.shape[0]], axis=0)
     key_count = piece_keys.shape[1]
     head_keys = piece_keys.reshape(slot_count, key_count, head_count, HEAD_DIM)
     head_values = piece_values.reshape(slot_count, key_count, head_count, HEAD_DIM)

time: 468 us -> 520 us (1.11)
  waiting for transfers between devices: 259 us -> 293 us
  local copies, waits for them, and re-layouts: 59.4 us -> 72 us
  other arithmetic: 47.2 us -> 52.7 us
    all_gather x2 -> x1, waiting for transfers between devices: 75.8 us -> 110 us  [cross_layer(): parts_out = lax.all_gather(wide_out, axis_name='seq', axis=1, tiled=True)]
    split x0 -> x2, local copies, waits for them, and re-layouts: none -> 24.9 us  [cross_layer(): piece_keys, piece_values = jnp.split(parts_out, [key_rows.shape[0]], axis=0)]
    all_gather x2 -> x0, local copies, waits for them, and re-layouts: 24.3 us -> none  [the longest x1 13 us: cross_layer(): piece_keys = lax.all_gather(key_rows, 'seq', axis=1, tiled=True)]
    unnamed x18 -> x22, local copies, waits for them, and re-layouts: 13.8 us -> 23.2 us
  transfers between devices with their start and end apart: 3 -> 2, of which waited for: 3 -> 2; matrix products, arithmetic and copies ran while one was open for 19% -> 8% of each run, Pallas kernels for 0% -> 0%
where the time goes in v1:
time: 520 us; the launch traced here: 519 us
  waiting for transfers between devices  293 us (56%)
  matrix products  81.2 us (16%)
  local copies, waits for them, and re-layouts  72 us (14%)
  other arithmetic  52.7 us (10%)
  between operations  13.6 us (3%)
  starting transfers between devices  6.96 us (1%)
    all_to_all x1, waiting for transfers between devices, regroup(): lax.all_to_all(outgoing, 'group', split_axis=0, concat_axis=0, tiled=True)  183 us
    all_gather x1, waiting for transfers between devices, cross_layer(): parts_out = lax.all_gather(wide_out, axis_name='seq', axis=1, tiled=True)  110 us
    split x2, local copies, waits for them, and re-layouts, cross_layer(): piece_keys, piece_values = jnp.split(parts_out, [key_rows.shape[0]], axis=0)  24.9 us
    dot_general x1, matrix products, cross_layer(): jnp.dot(context, w_out, preferred_element_type=jnp.float32)  23.7 us
    unnamed x22, local copies, waits for them, and re-layouts  23.2 us
    select_n x2, other arithmetic, spread_rows(): jnp.where(wanted[:, None, None], gathered, jnp.zeros((), source_array.dty...  22 us
    dot_general x1, matrix products, cross_layer(): jnp.einsum('sqhd,skhd->shqk', queries, head_keys, preferred_element_type=...  21.7 us
    gather x2, local copies, waits for them, and re-layouts, spread_rows(): gathered = jnp.take(source_array, source_index, axis=0)  20.9 us
  transfers between devices with their start and end apart: 2, of which 2 were waited for; matrix products, arithmetic and copies ran while one was open for 8% of the time, Pallas kernels for 0%

profile of v1, /device:TPU:0, one launch (start us, length us, event | category | flops | bytes accessed | tf_op | source)
XLA Modules:
  0.0 519.1 jit_solution(6655881202671598754)
XLA Ops:
  6.5 1.7 pad_maximum_fusion
  8.3 2.5 copy.28
  10.8 4.7 convert_reduce_fusion
  15.5 5.9 %fusion.4 = f32[8,256]{1,0:T(8,128)S(1)} fusion(bf16[8,256,2048]{2,1,0:T(8,128)(2,1)} %param.10, f32[8,256]{1,0:T(8,128)S(1)} %broadcast_multiply_fusion), kind=kLoop, calls=%fused_computation.10 | loop fusion | flops 16775168 | bytes 8404992 | tf_op jit(solution)/shard_map/reduce_sum | solution.py:38
  21.5 2.5 fusion.5
  24.0 0.4 slice-done.3
  24.4 19.4 %fusion.21 = bf16[256,8,16,128]{3,1,2,0:T(8,128)(2,1)} fusion(bf16[2048,2048]{1,0:T(8,128)(2,1)S(1)} %bitcast.29, bf16[2048,2048]{1,0:T(8,128)(2,1)S(1)} %bitcast.33), kind=kOutput, calls=%fused_computation.27 | convolution fusion | flops 17188257792 | bytes 25165824 | tf_op jit(solution)/shard_map/dot_general | solution.py:73
  43.8 9.9 %copy.39 = bf16[256,8,16,128]{3,2,1,0:T(8,128)(2,1)} copy(bf16[256,8,16,128]{3,1,2,0:T(8,128)(2,1)} %fusion.21) | data formatting | bytes 16777216
  53.9 0.2 select_reduce_fusion.4
  54.1 0.2 select_reduce_fusion.6
  54.8 109.9 %all-gather.2.cloned.1.call-done = bf16[16,256,2048]{2,0,1:T(8,128)(2,1)} async-done(((bf16[16,32,2048]{2,0,1:T(8,128)(2,1)}), bf16[16,256,2048]{2,0,1:T(8,128)(2,1)}) %all-gather.2.cloned.1.call-update) | async-done | bytes 16777232 | tf_op jit(solution)/shard_map/all_gather | solution.py:78
  164.8 12.0 %fusion.29 = (bf16[8,256,2048]{2,0,1:T(8,128)(2,1)}, bf16[8,256,2048]{2,0,1:T(8,128)(2,1)}) fusion(bf16[16,256,2048]{2,0,1:T(8,128)(2,1)} %all-gather.2.cloned.1.call-done), kind=kLoop, calls=%fused_computation.67 | loop fusion | bytes 33554432 | tf_op jit(solution)/shard_map/split | solution.py:79
  176.7 12.9 %copy.38 = bf16[8,256,2048]{1,2,0:T(8,128)(2,1)} copy(bf16[8,256,2048]{2,0,1:T(8,128)(2,1)} %get-tuple-element.16) | data formatting | bytes 16777216
  189.6 21.7 %select_reduce_fusion = (f32[8,16,256]{2,1,0:T(8,128)S(1)}, f32[8,16,256,256]{2,3,1,0:T(8,128)}) fusion(pred[8,256]{1,0:T(8,128)(4,1)S(1)} %iota_compare_fusion, bf16[8,256,16,128]{1,3,2,0:T(8,128)(2,1)} %bitcast.28, bf16[8,256,16,128]{3,2,1,0:T(8,128)(2,1)} %bitcast.27), kind=kOutput, calls=%fused_computation.3 | convolution fusion | flops 2164228096 | bytes 50464768 | tf_op jit(solution)/shard_map/sqhd,skhd->shqk/dot_general | solution.py:83
  211.3 12.9 %copy.32 = bf16[8,256,2048]{1,2,0:T(8,128)(2,1)} copy(bf16[8,256,2048]{2,0,1:T(8,128)(2,1)} %get-tuple-element.15) | data formatting | bytes 16777216 | tf_op jit(solution)/shard_map/split | solution.py:79
  224.2 15.0 %fusion = f32[8,16,256]{2,1,0:T(8,128)S(1)} fusion(f32[8,16,256,256]{2,3,1,0:T(8,128)} %get-tuple-element.20, f32[8,16,256]{2,1,0:T(8,128)S(1)} %broadcast_maximum_fusion, pred[8,256]{1,0:T(8,128)(4,1)S(1)} %iota_compare_fusion), kind=kLoop, calls=%fused_computation.4 | loop fusion | flops 33521664 | bytes 33818624 | tf_op jit(solution)/shard_map/reduce_sum | solution.py:89
  239.2 16.5 %fusion.8 = bf16[8,256,16,128]{1,3,2,0:T(8,128)(2,1)} fusion(f32[8,256,16]{1,2,0:T(8,128)S(1)} %bitcast.31, bf16[8,256,16,128]{1,3,2,0:T(8,128)(2,1)S(1)} %bitcast.30, f32[8,16,256,256]{2,3,1,0:T(8,128)} %get-tuple-element.20, f32[8,16,256]{2,1,0:T(8,128)S(1)} %broadcast_maximum_fusion, pred[8,256]{1,0:T(8,128)(4,1)S(1)} %iota_compare_fusion), kind=kOutput, calls=%fused_computation.14 | convolution fusion | flops 2189426688 | bytes 50595840 | tf_op jit(solution)/shard_map/shqk,skhd->shqd/dot_general | solution.py:91
  255.7 23.7 %select_convert_fusion = bf16[8,256,2048]{2,1,0:T(8,128)(2,1)} fusion(pred[8,256]{1,0:T(8,128)(4,1)S(1)} %broadcast_compare_fusion, bf16[8,256,2048]{1,2,0:T(8,128)(2,1)} %bitcast.34, bf16[2048,2048]{1,0:T(8,128)(2,1)} %param.19), kind=kOutput, calls=%fused_computation.16 | convolution fusion | flops 17188257792 | bytes 25167872 | tf_op jit(solution)/shard_map/dot_general | solution.py:101
  279.4 10.3 %gather_fusion = bf16[16,256,2048]{2,1,0:T(8,128)(2,1)} fusion(bf16[8,256,2048]{2,1,0:T(8,128)(2,1)} %select_convert_fusion, s32[1024]{0:T(1024)S(1)} %pad_clamp_fusion.1), kind=kCustom, calls=%fused_computation | custom fusion | bytes 33554496 | tf_op jit(solution)/shard_map/jit(_take)/gather | solution.py:43
  289.7 14.3 %select_select_fusion = bf16[16,256,2048]{2,1,0:T(8,128)(2,1)} fusion(bf16[16,256,2048]{2,1,0:T(8,128)(2,1)} %gather_fusion, pred[16]{0:T(512)(128)(4,1)S(1)} %compare_and_fusion.1, pred[16]{0:T(512)(128)(4,1)S(1)} %lt.144), kind=kLoop, calls=%fused_computation.15 | loop fusion | flops 16777216 | bytes 33554464 | tf_op jit(solution)/shard_map/jit(_where)/select_n | solution.py:44
  304.0 7.0 %all-to-all-start = ((bf16[16,256,2048]{2,1,0:T(8,128)(2,1)}), bf16[16,256,2048]{2,1,0:T(8,128)(2,1)}, u32[]{:S(2)}, u32[]{:S(2)}) async-start(bf16[16,256,2048]{2,1,0:T(8,128)(2,1)} %select_select_fusion), calls=%async_computation | async-start | bytes 33554432 | tf_op jit(solution)/shard_map/all_to_all | solution.py:60
  311.2 182.7 %all-to-all-done = bf16[16,256,2048]{2,1,0:T(8,128)(2,1)} async-done(((bf16[16,256,2048]{2,1,0:T(8,128)(2,1)}), bf16[16,256,2048]{2,1,0:T(8,128)(2,1)}, u32[]{:S(2)}, u32[]{:S(2)}) %all-to-all-start) | async-done | bytes 16777248 | tf_op jit(solution)/shard_map/all_to_all | solution.py:60
  493.9 10.6 %gather_fusion.1 = bf16[8,256,2048]{2,1,0:T(8,128)(2,1)} fusion(bf16[16,256,2048]{2,1,0:T(8,128)(2,1)} %all-to-all-done, s32[1024]{0:T(1024)S(1)} %pad_clamp_fusion), kind=kCustom, calls=%fused_computation.1 | custom fusion | bytes 16777248 | tf_op jit(solution)/shard_map/jit(_take)/gather | solution.py:43
  504.5 7.7 %select_select_fusion.1 = bf16[8,256,2048]{2,1,0:T(8,128)(2,1)} fusion(bf16[8,256,2048]{2,1,0:T(8,128)(2,1)} %gather_fusion.1, pred[8]{0:T(512)(128)(4,1)S(1)} %get-tuple-element.11, pred[8]{0:T(512)(128)(4,1)S(1)} %get-tuple-element.13), kind=kLoop, calls=%fused_computation.26 | loop fusion | flops 8388608 | bytes 16777232 | tf_op jit(solution)/shard_map/jit(_where)/select_n | solution.py:44
  (47 shorter events, 1.0 us)
Async XLA Ops:
  6.5 158.2 %all-gather.2.cloned.1.call-start = ((), (), s32[]{:S(2)}) async-start(), calls=%async_computation.1 | async-start | bytes 18874368 | tf_op jit(solution)/shard_map/all_gather | solution.py:78
  10.8 10.6 %slice-start = ((s8[8388608]{0:T(1024)(128)(4,1)}), s8[4194304]{0:T(1024)(128)(4,1)S(1)}, s32[]{:S(2)}) async-start(s8[8388608]{0:T(1024)(128)(4,1)} %bitcast.25), calls=%async_computation.2 | async-start | bytes 8388608
  15.5 5.9 %slice-start.1 = ((s8[8388608]{0:T(1024)(128)(4,1)}), s8[4194304]{0:T(1024)(128)(4,1)S(1)}, s32[]{:S(2)}) async-start(s8[8388608]{0:T(1024)(128)(4,1)} %bitcast.25), calls=%async_computation.3 | async-start | bytes 8388608
  15.5 8.5 %slice-start.2 = ((s8[8388608]{0:T(1024)(128)(4,1)}), s8[4194304]{0:T(1024)(128)(4,1)S(1)}, s32[]{:S(2)}) async-start(s8[8388608]{0:T(1024)(128)(4,1)} %bitcast.32), calls=%async_computation.4 | async-start | bytes 8388608
  21.5 3.0 slice-start.3
  43.8 9.9 %copy-start.4 = (s32[32]{0:T(128)S(1)}, s32[32]{0:T(128)}, u32[]{:S(2)}) copy-start(s32[32]{0:T(128)} %param.14) | copy-start | bytes 388
  43.8 10.0 %copy-start.5 = (s32[32]{0:T(128)S(1)}, s32[32]{0:T(128)}, u32[]{:S(2)}) copy-start(s32[32]{0:T(128)} %param.13) | copy-start | bytes 388
  43.8 10.1 %copy-start.1 = (s32[6]{0:T(128)S(1)}, s32[6]{0:T(128)}, u32[]{:S(2)}) copy-start(s32[6]{0:T(128)} %param.17) | copy-start | bytes 76
  43.8 10.1 %copy-start.2 = (s32[6]{0:T(128)S(1)}, s32[6]{0:T(128)}, u32[]{:S(2)}) copy-start(s32[6]{0:T(128)} %param.16) | copy-start | bytes 76
  43.8 10.1 %copy-start.3 = (s32[6]{0:T(128)S(1)}, s32[6]{0:T(128)}, u32[]{:S(2)}) copy-start(s32[6]{0:T(128)} %param.15) | copy-start | bytes 76
  224.2 15.0 %copy-start = (bf16[8,256,2048]{1,2,0:T(8,128)(2,1)S(1)}, bf16[8,256,2048]{1,2,0:T(8,128)(2,1)}, u32[]{:S(2)}) copy-start(bf16[8,256,2048]{1,2,0:T(8,128)(2,1)} %copy.32) | copy-start | bytes 25165828
  304.0 189.9 %all-to-all-start = ((bf16[16,256,2048]{2,1,0:T(8,128)(2,1)}), bf16[16,256,2048]{2,1,0:T(8,128)(2,1)}, u32[]{:S(2)}, u32[]{:S(2)}) async-start(bf16[16,256,2048]{2,1,0:T(8,128)(2,1)} %select_select_fusion), calls=%async_computation | async-start | bytes 33554432 | tf_op jit(solution)/shard_map/all_to_all | solution.py:60
Sparse Core Ops, SparseCore 0:
  10.9 153.7 all-gather.1
